TPU v7x, 32 devices: a whole 2x2x4 slice. The times are simulated.
32 devices in a mesh: cuts: 2 (over y), group: 16 (over z, x, core).
Axes of the slice: x: 2, y: 2, z: 4, core: 2. Of those that a mesh axis runs over, the one named last changes fastest.
Arguments:
- stem_blocks: bfloat16 [2, 64, 1024, 512], P('cuts', None, 'group'), may hold values from -6 to 6
- cap_tensor: bfloat16 [2, 2, 256, 256], P('cuts'), may hold values from -0.1875 to 0.1875
- slot_rows: int32 [64, 1024], P('group'), may hold values from 0 to 1023
- counts: int32 [64], P('group'), may hold values from 128 to 1024, as said below
Outputs:
- amplitudes: bfloat16 [1024, 64, 512], P('cuts', 'group')
Inputs may be any that keep to these rules, and one draw needn't show every extreme that they name: `counts`: some group has exactly 1024 live slots in every draw.
All inputs are finite; a program needn't handle non-finite values.
Results may differ from a plain program's by a relative error of at most 0.0052.
Values may be sent and summed in bfloat16 or wider, within the bound.
No kernel may reach another device: no remote copies, remote signals or barrier semaphores. Data moves between devices by JAX's collectives and lax.ppermute only.
A program may use at most 64 MiB of HBM per device.

v0:
```python
import jax
import jax.numpy as jnp
from jax import lax
from jax.sharding import PartitionSpec as P


def build_matrix(cap_pair):
    real_part = cap_pair[0]
    imag_part = cap_pair[1]
    upper = jnp.concatenate([real_part, imag_part], axis=1)
    lower = jnp.concatenate([-imag_part, real_part], axis=1)
    return jnp.concatenate([upper, lower], axis=0)


def local(stem_blocks, cap_tensor, slot_rows, counts):
    owned_rows = lax.all_to_all(stem_blocks[0], "group", split_axis=0, concat_axis=1, tiled=True)
    matrix = build_matrix(cap_tensor[0])
    slot_total = slot_rows.shape[1]
    share = slot_total // lax.axis_size("cuts")
    positions = jnp.arange(slot_total, dtype=jnp.int32)
    live_mask = positions[None, :] < counts[:, None]
    picked = jnp.take_along_axis(owned_rows, slot_rows[:, :, None], axis=1)
    product = jnp.einsum("gcr,rs->cgs", picked, matrix, preferred_element_type=jnp.float32)
    whole_sum = lax.psum(
        jnp.where(jnp.transpose(live_mask)[:, :, None], product, jnp.float32(0.0)).astype(
            jnp.bfloat16
        ),
        "cuts",
    ).astype(jnp.float32)
    summed = lax.dynamic_slice_in_dim(whole_sum, lax.axis_index("cuts") * share, share, 0)
    return summed.astype(jnp.bfloat16)


def solution(mesh):
    in_specs = (
        P("cuts", None, "group", None),
        P("cuts", None, None, None),
        P("group", None),
        P("group"),
    )
    out_specs = P("cuts", "group", None)
    return jax.shard_map(local, mesh=mesh, in_specs=in_specs, out_specs=out_specs, check_vma=False)
```

profile of v0, /device:TPU:0, one launch (start us, length us, event | category | flops | bytes accessed | tf_op | source)
XLA Modules:
  0.0 309.5 jit_solution(17406738748968861879)
XLA Ops:
  6.5 0.0 copy-start.1
  6.5 0.0 copy-start
  6.5 0.0 copy-start.2
  6.5 7.5 %all-to-all-start = ((bf16[64,64,512]{2,1,0:T(8,128)(2,1)}), bf16[64,64,512]{2,1,0:T(8,128)(2,1)}, u32[]{:S(2)}, u32[]{:S(2)}) async-start(bf16[64,64,512]{2,1,0:T(8,128)(2,1)} %bitcast.29), calls=%async_computation | async-start | bytes 8388608 | tf_op jit(solution)/shard_map/all_to_all | solution.py:16
  14.1 0.0 all-reduce.2.cloned.1.call-start
  14.1 0.0 copy-done.1
  14.2 0.0 copy-done
  14.2 0.1 copy.9
  14.3 0.1 copy.10
  14.4 0.0 copy-done.2
  14.4 0.1 iota_compare_fusion
  14.6 77.2 %all-to-all-done = bf16[64,64,512]{2,1,0:T(8,128)(2,1)} async-done(((bf16[64,64,512]{2,1,0:T(8,128)(2,1)}), bf16[64,64,512]{2,1,0:T(8,128)(2,1)}, u32[]{:S(2)}, u32[]{:S(2)}) %all-to-all-start) | async-done | bytes 4194336 | tf_op jit(solution)/shard_map/all_to_all | solution.py:16
  91.8 4.6 %copy.7 = bf16[16,4,64,512]{3,2,0,1:T(8,128)(2,1)} copy(bf16[16,4,64,512]{3,2,1,0:T(8,128)(2,1)} %bitcast.4) | data formatting | bytes 8388608 | tf_op jit(solution)/shard_map/all_to_all | solution.py:16
  96.4 72.6 %gather_fusion = bf16[4096,512]{1,0:T(8,128)(2,1)} fusion(bf16[4,1024,512]{2,1,0:T(8,128)(2,1)} %bitcast.26, s32[4096]{0:T(1024)S(1)} %bitcast.27), kind=kCustom, calls=%fused_computation | custom fusion | bytes 8421376 | tf_op jit(solution)/shard_map/jit(take_along_axis)/gather | solution.py:22
  169.0 5.8 %fusion = bf16[1024,4,512]{0,2,1:T(8,128)(2,1)} fusion(pred[1024,4]{0,1:T(4,128)(4,1)S(1)} %iota_compare_fusion, bf16[4,1024,512]{2,1,0:T(8,128)(2,1)} %bitcast.28, pred[4,1024]{1,0:T(4,128)(4,1)S(1)} %compare_and_fusion, bf16[256,256]{0,1:T(8,128)(2,1)S(1)} %bitcast.31, bf16[256,256]{0,1:T(8,128)(2,1)S(1)} %bitcast_negate_fusion, ...), kind=kOutput, calls=%fused_computation.2 | convolution fusion | flops 2155872256 | bytes 8790016 | tf_op jit(solution)/shard_map/gcr,rs->cgs/dot_general | solution.py:23
  174.8 0.0 all-reduce.2.cloned.1.call-update
  174.9 123.0 %all-reduce.2.cloned.1.call-done = bf16[1024,4,512]{0,2,1:T(8,128)(2,1)} async-done(((bf16[1024,4,512]{0,2,1:T(8,128)(2,1)}), bf16[1024,4,512]{0,2,1:T(8,128)(2,1)}) %all-reduce.2.cloned.1.call-update) | async-done | bytes 4194320 | tf_op jit(solution)/shard_map/psum | solution.py:24
  297.9 1.7 convert_convert_fusion
  299.6 3.1 copy.8
  (5 shorter events, 0.1 us)
Async XLA Ops:
  6.5 7.6 %copy-start.1 = (s32[4,1024]{1,0:T(4,128)S(1)}, s32[4,1024]{1,0:T(4,128)}, u32[]{:S(2)}) copy-start(s32[4,1024]{1,0:T(4,128)} %param.6) | copy-start | bytes 49156
  6.5 7.6 %copy-start = (bf16[1,2,256,256]{3,2,1,0:T(8,128)(2,1)S(1)}, bf16[1,2,256,256]{3,2,1,0:T(8,128)(2,1)}, u32[]{:S(2)}) copy-start(bf16[1,2,256,256]{3,2,1,0:T(8,128)(2,1)} %param.5) | copy-start | bytes 786436
  6.5 7.9 %copy-start.2 = (s32[4]{0:T(128)S(1)}, s32[4]{0:T(128)}, u32[]{:S(2)}) copy-start(s32[4]{0:T(128)} %param.7) | copy-start | bytes 52
  6.5 85.2 %all-to-all-start = ((bf16[64,64,512]{2,1,0:T(8,128)(2,1)}), bf16[64,64,512]{2,1,0:T(8,128)(2,1)}, u32[]{:S(2)}, u32[]{:S(2)}) async-start(bf16[64,64,512]{2,1,0:T(8,128)(2,1)} %bitcast.29), calls=%async_computation | async-start | bytes 8388608 | tf_op jit(solution)/shard_map/all_to_all | solution.py:16
  14.1 283.8 %all-reduce.2.cloned.1.call-start = ((), (), s32[]{:S(2)}) async-start(), calls=%async_computation.1 | async-start | bytes 8388608 | tf_op jit(solution)/shard_map/psum | solution.py:24
Sparse Core Ops, SparseCore 0:
  175.0 122.8 all-reduce.1
where the time goes:
time: 311 us; the launch traced here: 310 us
  waiting for transfers between devices  200 us (64%)
  local copies, waits for them, and re-layouts  80.5 us (26%)
  between operations  13.5 us (4%)
  starting transfers between devices  7.58 us (2%)
  matrix products  5.84 us (2%)
    psum x1, waiting for transfers between devices, local(): lax.psum(jnp.where(jnp.transpose(live_mask)[:, :, None], product, jnp.flo...  123 us
    all_to_all x1, waiting for transfers between devices, local(): lax.all_to_all(stem_blocks[0], 'group', split_axis=0, concat_axis=1, tile...  77.2 us
    gather x1, local copies, waits for them, and re-layouts, local(): picked = jnp.take_along_axis(owned_rows, slot_rows[:, :, None], axis=1)  72.6 us
    all_to_all x1, starting transfers between devices, local(): lax.all_to_all(stem_blocks[0], 'group', split_axis=0, concat_axis=1, tile...  7.54 us
  transfers between devices with their start and end apart: 2, of which 2 were waited for; matrix products, arithmetic and copies ran while one was open for 0% of the time, Pallas kernels for 0%

commit v1 on v0

--- a/solution.py
+++ b/solution.py
@@ -1,7 +1,16 @@
+import functools
 import jax
 import jax.numpy as jnp
 from jax import lax
 from jax.sharding import PartitionSpec as P
+
+
+def expand_the_block(local_block, mesh_name):
+    vec_out = lax.all_gather(local_block, mesh_name)
+    return jnp.sum(vec_out, 0)
+
+
+mark_surface_for = functools.partial(expand_the_block, mesh_name="cuts")
 
 
 def build_matrix(cap_pair):
@@ -21,11 +30,10 @@
     live_mask = positions[None, :] < counts[:, None]
     picked = jnp.take_along_axis(owned_rows, slot_rows[:, :, None], axis=1)
     product = jnp.einsum("gcr,rs->cgs", picked, matrix, preferred_element_type=jnp.float32)
-    whole_sum = lax.psum(
+    whole_sum = mark_surface_for(
         jnp.where(jnp.transpose(live_mask)[:, :, None], product, jnp.float32(0.0)).astype(
             jnp.bfloat16
-        ),
-        "cuts",
+        )
     ).astype(jnp.float32)
     summed = lax.dynamic_slice_in_dim(whole_sum, lax.axis_index("cuts") * share, share, 0)
     return summed.astype(jnp.bfloat16)

time: 311 us -> 345 us (1.11)
  other arithmetic: 1.84 us -> 25.6 us
  local copies, waits for them, and re-layouts: 80.5 us -> 95 us
  waiting for transfers between devices: 200 us -> 196 us
    psum x1 -> x0, waiting for transfers between devices: 123 us -> none  [local(): lax.psum(jnp.where(jnp.transpose(live_mask)[:, :, None], product, jnp.flo...]
    all_gather x0 -> x1, waiting for transfers between devices: none -> 119 us  [expand_the_block(): vec_out = lax.all_gather(local_block, mesh_name)]
    reduce_sum x0 -> x1, other arithmetic: none -> 23.8 us  [expand_the_block(): return jnp.sum(vec_out, 0)]
    all_gather x0 -> x1, local copies, waits for them, and re-layouts: none -> 14.5 us  [expand_the_block(): vec_out = lax.all_gather(local_block, mesh_name)]
where the time goes in v1:
time: 345 us; the launch traced here: 344 us
  waiting for transfers between devices  196 us (57%)
  local copies, waits for them, and re-layouts  95 us (28%)
  other arithmetic  25.6 us (7%)
  between operations  13.5 us (4%)
  starting transfers between devices  7.58 us (2%)
  matrix products  5.77 us (2%)
    all_gather x1, waiting for transfers between devices, expand_the_block(): vec_out = lax.all_gather(local_block, mesh_name)  119 us
    all_to_all x1, waiting for transfers between devices, local(): lax.all_to_all(stem_blocks[0], 'group', split_axis=0, concat_axis=1, tile...  77.2 us
    gather x1, local copies, waits for them, and re-layouts, local(): picked = jnp.take_along_axis(owned_rows, slot_rows[:, :, None], axis=1)  72.6 us
    reduce_sum x1, other arithmetic, expand_the_block(): return jnp.sum(vec_out, 0)  23.8 us
    all_gather x1, local copies, waits for them, and re-layouts, expand_the_block(): vec_out = lax.all_gather(local_block, mesh_name)  14.5 us
    all_to_all x1, starting transfers between devices, local(): lax.all_to_all(stem_blocks[0], 'group', split_axis=0, concat_axis=1, tile...  7.54 us
  transfers between devices with their start and end apart: 2, of which 2 were waited for; matrix products, arithmetic and copies ran while one was open for 0% of the time, Pallas kernels for 0%

profile of v1, /device:TPU:0, one launch (start us, length us, event | category | flops | bytes accessed | tf_op | source)
XLA Modules:
  0.0 343.9 jit_solution(17121655279956932710)
XLA Ops:
  6.5 0.0 copy-start.1
  6.5 0.0 copy-start
  6.5 0.0 copy-start.2
  6.5 7.5 %all-to-all-start = ((bf16[64,64,512]{2,1,0:T(8,128)(2,1)}), bf16[64,64,512]{2,1,0:T(8,128)(2,1)}, u32[]{:S(2)}, u32[]{:S(2)}) async-start(bf16[64,64,512]{2,1,0:T(8,128)(2,1)} %bitcast.31), calls=%async_computation | async-start | bytes 8388608 | tf_op jit(solution)/shard_map/all_to_all | solution.py:25
  14.1 0.0 all-gather.3.cloned.1.call-start
  14.1 0.0 copy-done.1
  14.2 0.0 copy-done
  14.2 0.1 copy.12
  14.3 0.1 copy.13
  14.4 0.0 copy-done.2
  14.4 0.1 iota_compare_fusion
  14.6 77.2 %all-to-all-done = bf16[64,64,512]{2,1,0:T(8,128)(2,1)} async-done(((bf16[64,64,512]{2,1,0:T(8,128)(2,1)}), bf16[64,64,512]{2,1,0:T(8,128)(2,1)}, u32[]{:S(2)}, u32[]{:S(2)}) %all-to-all-start) | async-done | bytes 4194336 | tf_op jit(solution)/shard_map/all_to_all | solution.py:25
  91.8 4.6 %copy.10 = bf16[16,4,64,512]{3,2,0,1:T(8,128)(2,1)} copy(bf16[16,4,64,512]{3,2,1,0:T(8,128)(2,1)} %bitcast.4) | data formatting | bytes 8388608 | tf_op jit(solution)/shard_map/all_to_all | solution.py:25
  96.4 72.6 %gather_fusion = bf16[4096,512]{1,0:T(8,128)(2,1)} fusion(bf16[4,1024,512]{2,1,0:T(8,128)(2,1)} %bitcast.28, s32[4096]{0:T(1024)S(1)} %bitcast.29), kind=kCustom, calls=%fused_computation | custom fusion | bytes 8421376 | tf_op jit(solution)/shard_map/jit(take_along_axis)/gather | solution.py:31
  169.0 5.8 %fusion = bf16[1024,4,512]{0,2,1:T(8,128)(2,1)} fusion(pred[1024,4]{0,1:T(4,128)(4,1)S(1)} %iota_compare_fusion, bf16[4,1024,512]{2,1,0:T(8,128)(2,1)} %bitcast.30, pred[4,1024]{1,0:T(4,128)(4,1)S(1)} %compare_and_fusion, bf16[256,256]{0,1:T(8,128)(2,1)S(1)} %bitcast.33, bf16[256,256]{0,1:T(8,128)(2,1)S(1)} %bitcast_negate_fusion, ...), kind=kOutput, calls=%fused_computation.2 | convolution fusion | flops 2155872256 | bytes 8790016 | tf_op jit(solution)/shard_map/gcr,rs->cgs/dot_general | solution.py:32
  174.8 0.0 all-gather.3.cloned.1.call-update
  174.8 119.2 %all-gather.3.cloned.1.call-done = bf16[2048,4,512]{0,2,1:T(8,128)(2,1)} async-done(((bf16[1024,4,512]{0,2,1:T(8,128)(2,1)}), bf16[2048,4,512]{0,2,1:T(8,128)(2,1)}) %all-gather.3.cloned.1.call-update) | async-done | bytes 8388624 | tf_op jit(solution)/shard_map/all_gather | solution.py:9
  294.0 14.5 %reshape.36 = bf16[2,1024,4,512]{1,0,3,2:T(2,128)(2,1)} reshape(bf16[2048,4,512]{0,2,1:T(8,128)(2,1)} %all-gather.3.cloned.1.call-done) | data formatting | bytes 16777216 | tf_op jit(solution)/shard_map/all_gather | solution.py:9
  308.5 23.8 %reduce_sum.12 = bf16[1024,4,512]{0,2,1:T(8,128)(2,1)} reduce(bf16[2,1024,4,512]{1,0,3,2:T(2,128)(2,1)} %reshape.36, bf16[]{:T(256)} %constant.24.clone.1), dimensions={0}, to_apply=%region_0.0 | reduce | flops 2097152 | bytes 12582914 | tf_op jit(solution)/shard_map/reduce_sum | solution.py:10
  332.3 1.7 convert_convert_fusion
  334.0 3.1 copy.11
  (5 shorter events, 0.1 us)
Async XLA Ops:
  6.5 7.6 %copy-start.1 = (s32[4,1024]{1,0:T(4,128)S(1)}, s32[4,1024]{1,0:T(4,128)}, u32[]{:S(2)}) copy-start(s32[4,1024]{1,0:T(4,128)} %param.6) | copy-start | bytes 49156
  6.5 7.6 %copy-start = (bf16[1,2,256,256]{3,2,1,0:T(8,128)(2,1)S(1)}, bf16[1,2,256,256]{3,2,1,0:T(8,128)(2,1)}, u32[]{:S(2)}) copy-start(bf16[1,2,256,256]{3,2,1,0:T(8,128)(2,1)} %param.5) | copy-start | bytes 786436
  6.5 7.9 %copy-start.2 = (s32[4]{0:T(128)S(1)}, s32[4]{0:T(128)}, u32[]{:S(2)}) copy-start(s32[4]{0:T(128)} %param.7) | copy-start | bytes 52
  6.5 85.2 %all-to-all-start = ((bf16[64,64,512]{2,1,0:T(8,128)(2,1)}), bf16[64,64,512]{2,1,0:T(8,128)(2,1)}, u32[]{:S(2)}, u32[]{:S(2)}) async-start(bf16[64,64,512]{2,1,0:T(8,128)(2,1)} %bitcast.31), calls=%async_computation | async-start | bytes 8388608 | tf_op jit(solution)/shard_map/all_to_all | solution.py:25
  14.1 279.9 %all-gather.3.cloned.1.call-start = ((), (), s32[]{:S(2)}) async-start(), calls=%async_computation.1 | async-start | bytes 12582912 | tf_op jit(solution)/shard_map/all_gather | solution.py:9
Sparse Core Ops, SparseCore 0:
  174.9 119.0 all-gather.2
